TPU v7x, 128 devices: a whole 4x4x4 slice. The times are simulated.
128 devices in a mesh: seq: 32 (over y_lo, z, x), head: 4 (over y_hi, core).
Axes of the slice: x: 4, y: 4 (y_hi: 2, y_lo: 2; y = y_hi * 2 + y_lo), z: 4, core: 2. Of those that a mesh axis runs over, the one named last changes fastest.
Arguments:
- tokens: bfloat16 [4096, 7168], P('seq', 'head'), may hold values from -6 to 6
- latent_down: bfloat16 [7168, 576], P('head'), may hold values from -0.0625 to 0.0625
- latent_gain: float32 [512], replicated, may hold values from 0.5 to 1.5
- query_nope: bfloat16 [4096, 8192], P('seq', 'head'), may hold values from -200 to 200
- query_rope: bfloat16 [4096, 4096], P('seq', 'head'), may hold values from -6 to 6
- key_up: bfloat16 [64, 128, 512], P('head'), may hold values from -0.5 to 0.5
- value_up: bfloat16 [64, 512, 128], P('head'), may hold values from -0.25 to 0.25
- prefix_latent: bfloat16 [2048, 576], P('seq'), may hold values from -6 to 6
- prefix_length: int32 [1], replicated, may hold values from 1024 to 2048
- page_table: int32 [256], replicated, may hold values from 0 to 255, each once
Outputs:
- attended: bfloat16 [4096, 8192], P('seq', 'head')
- decode_pool: bfloat16 [256, 9216], P('seq')
Inputs may be any that keep to these rules, and one draw needn't show every extreme that they name: The prefix rows from prefix_length[0] on are not live. `page_table`: A permutation of the 256 decode slots.
All inputs are finite; a program needn't handle non-finite values.
Results may differ from a plain program's by a relative error of at most 0.015.
Values may be sent and summed in bfloat16 or wider, within the bound.
A program may use at most 128 MiB of HBM per device.

v0:
```python
import jax
import jax.numpy as jnp
from jax import lax
from jax.sharding import PartitionSpec as P

LATENT = 512
ROPE = 64
NOPE = 128
VHEAD = 128
PAGE = 16


def sent_to_all(value, axis):
    copies = jnp.broadcast_to(value, (lax.axis_size(axis), *value.shape))
    return lax.all_to_all(copies, axis, split_axis=0, concat_axis=0, tiled=True)


def of_everyone(value, axis):
    return sent_to_all(value, axis).astype(jnp.float32).sum(axis=0)


def in_order(parts, dim):
    lengths = list(parts.shape[1:])
    lengths[dim] *= parts.shape[0]
    return jnp.moveaxis(parts, 0, dim).reshape(lengths)


def gather_directly(value, axis, dim):
    parts = sent_to_all(value, axis)
    return in_order(parts, dim)


def angles(positions):
    half_width = ROPE // 2
    frequency = 10000.0 ** (-jnp.arange(half_width, dtype=jnp.float32) / half_width)
    return positions.astype(jnp.float32)[:, None] * frequency[None, :]


def rotate(values, angle_table):
    half_width = values.shape[-1] // 2
    first = values[..., :half_width]
    second = values[..., half_width:]
    cosine = jnp.cos(angle_table)
    sinus = jnp.sin(angle_table)
    return jnp.concatenate(
        [first * cosine - second * sinus, first * sinus + second * cosine], axis=-1
    )


def finish(mixed, latent_gain, positions):
    latent = mixed[:, :LATENT]
    rope_part = mixed[:, LATENT:]
    normed = (
        latent * lax.rsqrt(jnp.mean(latent * latent, axis=1, keepdims=True) + 1e-06) * latent_gain
    )
    return jnp.concatenate(
        [normed.astype(jnp.bfloat16), rotate(rope_part, angles(positions)).astype(jnp.bfloat16)],
        axis=1,
    )


def per_device(
    tokens,
    latent_down,
    latent_gain,
    query_nope,
    query_rope,
    key_up,
    value_up,
    prefix_latent,
    prefix_length,
    page_table,
):
    row_count = tokens.shape[0]
    head_count = key_up.shape[0]
    row_width = LATENT + ROPE
    queries_dev = row_count * head_count
    seq_index = lax.axis_index("seq")
    offset = prefix_length[0]
    first_row = seq_index * row_count
    positions = offset + first_row + jnp.arange(row_count, dtype=jnp.int32)
    partial_terms = jnp.dot(tokens, latent_down, preferred_element_type=jnp.float32)
    mixed = of_everyone(partial_terms.astype(jnp.bfloat16), "head").astype(jnp.float32)
    new_keys = finish(mixed, latent_gain, positions)
    lifted = jnp.einsum(
        "thn,hnl->thl",
        query_nope.reshape(row_count, head_count, NOPE),
        key_up,
        preferred_element_type=jnp.float32,
    ).astype(jnp.bfloat16)
    turned = rotate(
        query_rope.reshape(row_count, head_count, ROPE).astype(jnp.float32),
        angles(positions)[:, None, :],
    ).astype(jnp.bfloat16)
    queries = jnp.concatenate([lifted, turned], axis=2).reshape(queries_dev, row_width)
    query_token = first_row + jnp.arange(queries_dev, dtype=jnp.int32) // head_count
    score_scale = (NOPE + ROPE) ** (-0.5)

    def attend(state, key_rows, live_mask):
        running_top, denominator, running = state
        scores = (
            lax.dot_general(
                key_rows, queries, (((1,), (1,)), ((), ())), preferred_element_type=jnp.float32
            )
            * score_scale
        )
        new_top = jnp.maximum(running_top, jnp.max(jnp.where(live_mask, scores, -1e30), axis=0))
        weights = jnp.where(live_mask, jnp.exp(scores - new_top[None, :]), 0.0)
        fading = jnp.exp(running_top - new_top)
        denominator = denominator * fading + jnp.sum(weights, axis=0)
        update = lax.dot_general(
            weights.astype(jnp.bfloat16),
            key_rows[:, :LATENT],
            (((0,), (0,)), ((), ())),
            preferred_element_type=jnp.float32,
        )
        return (new_top, denominator, running * fading[:, None] + update)

    def guarded(state, key_rows, live_mask):
        return attend(state, key_rows, live_mask)

    def sweep_keys(state, key_rows, live_rule):
        total_rows = key_rows.shape[0]
        blocks = key_rows.reshape(total_rows // 512, 512, row_width)
        starts = 512 * jnp.arange(total_rows // 512, dtype=jnp.int32)

        def advance(inner_state, block_pair):
            key_block, block_start = block_pair
            key_index = block_start + jnp.arange(512, dtype=jnp.int32)
            return (guarded(inner_state, key_block, live_rule(key_index)), None)

        state, unused = lax.scan(advance, state, (blocks, starts))
        return state

    def prefix_rule(key_index):
        return jnp.broadcast_to((key_index < offset)[:, None], (key_index.shape[0], queries_dev))

    def group_rule(key_index):
        return key_index[:, None] <= query_token[None, :]

    prefix_all = gather_directly(prefix_latent, "seq", 0)
    state = (
        jnp.full((queries_dev,), -1e30, jnp.float32),
        jnp.zeros((queries_dev,), jnp.float32),
        jnp.zeros((queries_dev, LATENT), jnp.float32),
    )
    state = sweep_keys(state, prefix_all, prefix_rule)
    pages_dev = row_count // PAGE
    page_width = PAGE * row_width
    all_keys = lax.all_gather(new_keys, "seq", axis=0, tiled=True)
    state = sweep_keys(state, all_keys, group_rule)
    axis_size = lax.axis_size("seq")
    targets = lax.dynamic_slice_in_dim(page_table, seq_index * pages_dev, pages_dev)
    slot_ids = jnp.arange(axis_size * pages_dev, dtype=jnp.int32)
    select = (slot_ids[:, None] == targets[None, :]).astype(jnp.bfloat16)
    outgoing = jnp.dot(
        select, new_keys.reshape(pages_dev, page_width), preferred_element_type=jnp.float32
    ).astype(jnp.bfloat16)
    incoming = lax.all_to_all(outgoing, "seq", split_axis=0, concat_axis=0, tiled=True)
    decode_pool = jnp.sum(
        incoming.reshape(axis_size, pages_dev, page_width), axis=0, dtype=jnp.float32
    )
    running_top, denominator, running = state
    attention = (
        (running / denominator[:, None]).astype(jnp.bfloat16).reshape(row_count, head_count, LATENT)
    )
    output = jnp.einsum("thl,hlv->thv", attention, value_up, preferred_element_type=jnp.float32)
    attended = output.astype(jnp.bfloat16).reshape(row_count, head_count * VHEAD)
    return (attended, decode_pool.astype(jnp.bfloat16))


def solution(mesh):
    placed = (
        P("seq", "head"),
        P("head", None),
        P(),
        P("seq", "head"),
        P("seq", "head"),
        P("head", None, None),
        P("head", None, None),
        P("seq", None),
        P(),
        P(),
    )
    return jax.shard_map(
        per_device,
        mesh=mesh,
        in_specs=placed,
        out_specs=(P("seq", "head"), P("seq", None)),
        check_vma=False,
    )
```

profile of v0, /device:TPU:32, one launch (start us, length us, event | category | flops | bytes accessed | tf_op | source)
XLA Modules:
  0.0 342.1 jit_solution(6677885738440692457)
XLA Ops:
  7.2 2.6 convolution_convert_fusion.1
  10.7 4.5 %all-to-all-start.1 = ((bf16[4,128,576]{1,2,0:T(8,128)(2,1)}), bf16[4,128,576]{1,2,0:T(8,128)(2,1)S(1)}, u32[]{:S(2)}, u32[]{:S(2)}) async-start(bf16[4,128,576]{1,2,0:T(8,128)(2,1)} %broadcast_in_dim.54), calls=%async_computation.1 | async-start | bytes 1179648 | tf_op jit(solution)/shard_map/all_to_all | solution.py:15
  16.0 10.1 %all-to-all-done.1 = bf16[4,128,576]{1,2,0:T(8,128)(2,1)S(1)} async-done(((bf16[4,128,576]{1,2,0:T(8,128)(2,1)}), bf16[4,128,576]{1,2,0:T(8,128)(2,1)S(1)}, u32[]{:S(2)}, u32[]{:S(2)}) %all-to-all-start.1) | async-done | bytes 589856 | tf_op jit(solution)/shard_map/all_to_all | solution.py:15
  26.2 2.7 broadcast_in_dim.53
  28.9 8.2 %all-to-all-start = ((bf16[32,64,576]{2,1,0:T(8,128)(2,1)}), bf16[32,64,576]{2,1,0:T(8,128)(2,1)}, u32[]{:S(2)}, u32[]{:S(2)}) async-start(bf16[32,64,576]{2,1,0:T(8,128)(2,1)} %broadcast_in_dim.53), calls=%async_computation | async-start | bytes 5242880 | tf_op jit(solution)/shard_map/all_to_all | solution.py:15
  37.2 3.2 convert_bitcast_fusion
  41.6 1.1 copy.46
  42.7 3.2 pad_maximum_fusion
  45.9 4.9 %copy.42 = bf16[128,16,576]{2,1,0:T(8,128)(2,1)} copy(bf16[128,16,576]{0,2,1:T(8,128)(2,1)} %pad_maximum_fusion) | data formatting | bytes 4718592 | tf_op jit(solution)/shard_map/concatenate | solution.py:95
  51.0 3.5 %fusion.30 = bf16[32,8,9216]{2,1,0:T(8,128)(2,1)} fusion(bf16[8,9216]{1,0:T(8,128)(2,1)S(1)} %reshape.119, s32[8]{0:T(128)S(1)} %dynamic_slice.19), kind=kOutput, calls=%fused_computation.47 | convolution fusion | flops 40110080 | bytes 4866080 | tf_op jit(solution)/shard_map/dot_general | solution.py:156
  54.4 20.2 %all-to-all-done = bf16[32,64,576]{2,1,0:T(8,128)(2,1)} async-done(((bf16[32,64,576]{2,1,0:T(8,128)(2,1)}), bf16[32,64,576]{2,1,0:T(8,128)(2,1)}, u32[]{:S(2)}, u32[]{:S(2)}) %all-to-all-start) | async-done | bytes 2359328 | tf_op jit(solution)/shard_map/all_to_all | solution.py:15
  74.6 7.5 %all-to-all-start.2 = ((bf16[32,8,9216]{2,1,0:T(8,128)(2,1)}), bf16[32,8,9216]{2,1,0:T(8,128)(2,1)}, u32[]{:S(2)}, u32[]{:S(2)}) async-start(bf16[32,8,9216]{2,1,0:T(8,128)(2,1)} %fusion.30), calls=%async_computation.2 | async-start | bytes 9437184 | tf_op jit(solution)/shard_map/all_to_all | solution.py:159
  82.1 65.6 %while.31 = (s32[]{:T(128)}, f32[2048]{0:T(1024)S(1)}, f32[2048]{0:T(1024)S(1)}, f32[2048,512]{1,0:T(8,128)}, s32[4]{0:T(128)S(1)}, /*index=5*/s32[]{:T(128)}, b...) while((s32[]{:T(128)}, f32[2048]{0:T(1024)S(1)}, ...), condition=%wide.region_3.4_spmd.clone, body=%wide.region_0.3_spmd.clone.sunk | while | flops 2296392704 | bytes 42535076 | solution.py:132
  82.7 1.2 add_compare_fusion.2
  83.9 1.2 dynamic-slice_bitcast_fusion.5
  85.1 5.7 %select_reduce_fusion.2 = (f32[2048]{0:T(1024)S(1)}, f32[512,2048]{1,0:T(8,128)}) fusion(pred[512]{0:T(512)(128)(4,1)S(1)} %add_compare_fusion.2, bf16[512,576]{1,0:T(8,128)(2,1)S(1)} %dynamic-slice_bitcast_fusion.5, bf16[2048,576]{1,0:T(8,128)(2,1)} %get-tuple-element.343), kind=kOutput, calls=%fused_computation.30.clone.1 | convolution fusion | flops 1211103232 | bytes 7152128 | tf_op jit(solution)/shard_map/while/body/eval_jaxpr/dot_general | solution.py:102
  90.8 3.2 fusion.74
  94.3 3.1 fusion.76
  97.9 1.2 add_compare_fusion.2
  99.1 1.2 dynamic-slice_bitcast_fusion.5
  100.3 5.7 %select_reduce_fusion.2 = (f32[2048]{0:T(1024)S(1)}, f32[512,2048]{1,0:T(8,128)}) fusion(pred[512]{0:T(512)(128)(4,1)S(1)} %add_compare_fusion.2, bf16[512,576]{1,0:T(8,128)(2,1)S(1)} %dynamic-slice_bitcast_fusion.5, bf16[2048,576]{1,0:T(8,128)(2,1)} %get-tuple-element.343), kind=kOutput, calls=%fused_computation.30.clone.1 | convolution fusion | flops 1211103232 | bytes 7152128 | tf_op jit(solution)/shard_map/while/body/eval_jaxpr/dot_general | solution.py:102
  106.0 3.2 fusion.74
  109.5 4.7 %fusion.76 = f32[2048,512]{1,0:T(8,128)} fusion(f32[2048,512]{1,0:T(8,128)} %get-tuple-element.329, f32[512,2048]{1,0:T(8,128)S(1)} %copy-done.1, f32[2048]{0:T(1024)S(1)} %get-tuple-element.315, f32[2048]{0:T(1024)S(1)} %select_maximum_fusion.2, pred[512]{0:T(512)(128)(4,1)S(1)} %add_compare_fusion.2, pred[]{:T(512)S(6)} %compare.5, ...), kind=kOutput, calls=%fused_computation.28.clone.1 | convolution fusion | flops 1081081856 | bytes 13124097 | tf_op jit(solution)/shard_map/while/body/eval_jaxpr/dot_general | solution.py:111
  114.7 1.2 add_compare_fusion.2
  115.9 1.2 dynamic-slice_bitcast_fusion.5
  117.1 5.7 %select_reduce_fusion.2 = (f32[2048]{0:T(1024)S(1)}, f32[512,2048]{1,0:T(8,128)}) fusion(pred[512]{0:T(512)(128)(4,1)S(1)} %add_compare_fusion.2, bf16[512,576]{1,0:T(8,128)(2,1)S(1)} %dynamic-slice_bitcast_fusion.5, bf16[2048,576]{1,0:T(8,128)(2,1)} %get-tuple-element.343), kind=kOutput, calls=%fused_computation.30.clone.1 | convolution fusion | flops 1211103232 | bytes 7152128 | tf_op jit(solution)/shard_map/while/body/eval_jaxpr/dot_general | solution.py:102
  122.8 3.2 fusion.74
  126.2 4.7 %fusion.76 = f32[2048,512]{1,0:T(8,128)} fusion(f32[2048,512]{1,0:T(8,128)} %get-tuple-element.329, f32[512,2048]{1,0:T(8,128)S(1)} %copy-done.1, f32[2048]{0:T(1024)S(1)} %get-tuple-element.315, f32[2048]{0:T(1024)S(1)} %select_maximum_fusion.2, pred[512]{0:T(512)(128)(4,1)S(1)} %add_compare_fusion.2, pred[]{:T(512)S(6)} %compare.5, ...), kind=kOutput, calls=%fused_computation.28.clone.1 | convolution fusion | flops 1081081856 | bytes 13124097 | tf_op jit(solution)/shard_map/while/body/eval_jaxpr/dot_general | solution.py:111
  131.5 1.2 add_compare_fusion.2
  132.7 1.2 dynamic-slice_bitcast_fusion.5
  133.8 5.7 %select_reduce_fusion.2 = (f32[2048]{0:T(1024)S(1)}, f32[512,2048]{1,0:T(8,128)}) fusion(pred[512]{0:T(512)(128)(4,1)S(1)} %add_compare_fusion.2, bf16[512,576]{1,0:T(8,128)(2,1)S(1)} %dynamic-slice_bitcast_fusion.5, bf16[2048,576]{1,0:T(8,128)(2,1)} %get-tuple-element.343), kind=kOutput, calls=%fused_computation.30.clone.1 | convolution fusion | flops 1211103232 | bytes 7152128 | tf_op jit(solution)/shard_map/while/body/eval_jaxpr/dot_general | solution.py:102
  139.6 3.2 fusion.74
  143.1 4.7 %fusion.76 = f32[2048,512]{1,0:T(8,128)} fusion(f32[2048,512]{1,0:T(8,128)} %get-tuple-element.329, f32[512,2048]{1,0:T(8,128)S(1)} %copy-done.1, f32[2048]{0:T(1024)S(1)} %get-tuple-element.315, f32[2048]{0:T(1024)S(1)} %select_maximum_fusion.2, pred[512]{0:T(512)(128)(4,1)S(1)} %add_compare_fusion.2, pred[]{:T(512)S(6)} %compare.5, ...), kind=kOutput, calls=%fused_computation.28.clone.1 | convolution fusion | flops 1081081856 | bytes 13124097 | tf_op jit(solution)/shard_map/while/body/eval_jaxpr/dot_general | solution.py:111
  147.7 6.9 %all-to-all-done.2 = bf16[32,8,9216]{2,1,0:T(8,128)(2,1)} async-done(((bf16[32,8,9216]{2,1,0:T(8,128)(2,1)}), bf16[32,8,9216]{2,1,0:T(8,128)(2,1)}, u32[]{:S(2)}, u32[]{:S(2)}) %all-to-all-start.2) | async-done | bytes 4718624 | tf_op jit(solution)/shard_map/all_to_all | solution.py:159
  154.6 3.7 %reduce_sum.50 = bf16[8,9216]{1,0:T(8,128)(2,1)} reduce(bf16[32,8,9216]{2,1,0:T(8,128)(2,1)} %all-to-all-done.2, bf16[]{:T(256)} %constant.81.clone.1), dimensions={0}, to_apply=%region_10.11 | reduce | flops 2285568 | bytes 4866050 | tf_op jit(solution)/shard_map/reduce_sum | solution.py:160
  158.4 69.1 %all-gather.2.cloned.1.call-done = bf16[4096,576]{0,1:T(8,128)(2,1)} async-done(((bf16[128,576]{0,1:T(8,128)(2,1)}), bf16[4096,576]{0,1:T(8,128)(2,1)}) %all-gather.2.cloned.1.call-update) | async-done | bytes 4718608 | tf_op jit(solution)/shard_map/all_gather | solution.py:150
  227.5 7.6 %copy.50 = bf16[4096,576]{1,0:T(8,128)(2,1)} copy(bf16[4096,576]{0,1:T(8,128)(2,1)} %all-gather.2.cloned.1.call-done) | data formatting | bytes 9437184
  235.1 93.6 %while.30 = (s32[]{:T(128)}, f32[2048]{0:T(1024)S(1)}, f32[2048]{0:T(1024)S(1)}, f32[2048,512]{1,0:T(8,128)}, s32[8]{0:T(128)S(1)}, /*index=5*/bf16[8,512,576]{2...) while((s32[]{:T(128)}, f32[2048]{0:T(1024)S(1)}, f32[2048]{0:T(1024)S(1)}, ...), condition=%wide.region_9.10_spmd.clone, body=%wide.region_6.9_spmd.clone.sunk | while | flops 2298501632 | bytes 25796724 | solution.py:132
  236.3 1.2 dynamic-slice_bitcast_fusion.4
  237.5 3.6 %fusion.68 = (f32[2048]{0:T(1024)S(1)}, f32[512,2048]{1,0:T(8,128)S(1)}) fusion(s32[2048]{0:T(1024)S(1)} %fusion.67, s32[512]{0:T(512)S(1)} %iota_add_fusion.2, bf16[512,576]{1,0:T(8,128)(2,1)S(1)} %dynamic-slice_bitcast_fusion.4, bf16[2048,576]{1,0:T(8,128)(2,1)} %get-tuple-element.370), kind=kOutput, calls=%fused_computation.3.clone.1 | convolution fusion | flops 1212151808 | bytes 7161856 | tf_op jit(solution)/shard_map/while/body/eval_jaxpr/dot_general | solution.py:102
  242.2 4.6 %multiply_add_fusion.5 = f32[2048,512]{1,0:T(8,128)} fusion(f32[2048,512]{1,0:T(8,128)} %get-tuple-element.358, f32[512,2048]{1,0:T(8,128)S(1)} %get-tuple-element.301, f32[2048]{0:T(1024)S(1)} %get-tuple-element.303, f32[2048]{0:T(1024)S(1)} %max.11, s32[2048]{0:T(1024)S(1)} %fusion.67, s32[512]{0:T(512)S(1)} %iota_add_fusion.2, ...), kind=kOutput, calls=%fused_computation.4.clone.1 | convolution fusion | flops 1081081856 | bytes 13133824 | tf_op jit(solution)/shard_map/while/body/eval_jaxpr/dot_general | solution.py:111
  248.0 1.2 dynamic-slice_bitcast_fusion.4
  249.2 3.7 %fusion.68 = (f32[2048]{0:T(1024)S(1)}, f32[512,2048]{1,0:T(8,128)S(1)}) fusion(s32[2048]{0:T(1024)S(1)} %fusion.67, s32[512]{0:T(512)S(1)} %iota_add_fusion.2, bf16[512,576]{1,0:T(8,128)(2,1)S(1)} %dynamic-slice_bitcast_fusion.4, bf16[2048,576]{1,0:T(8,128)(2,1)} %get-tuple-element.370), kind=kOutput, calls=%fused_computation.3.clone.1 | convolution fusion | flops 1212151808 | bytes 7161856 | tf_op jit(solution)/shard_map/while/body/eval_jaxpr/dot_general | solution.py:102
  253.9 4.6 %multiply_add_fusion.5 = f32[2048,512]{1,0:T(8,128)} fusion(f32[2048,512]{1,0:T(8,128)} %get-tuple-element.358, f32[512,2048]{1,0:T(8,128)S(1)} %get-tuple-element.301, f32[2048]{0:T(1024)S(1)} %get-tuple-element.303, f32[2048]{0:T(1024)S(1)} %max.11, s32[2048]{0:T(1024)S(1)} %fusion.67, s32[512]{0:T(512)S(1)} %iota_add_fusion.2, ...), kind=kOutput, calls=%fused_computation.4.clone.1 | convolution fusion | flops 1081081856 | bytes 13133824 | tf_op jit(solution)/shard_map/while/body/eval_jaxpr/dot_general | solution.py:111
  259.7 1.2 dynamic-slice_bitcast_fusion.4
  260.9 3.6 %fusion.68 = (f32[2048]{0:T(1024)S(1)}, f32[512,2048]{1,0:T(8,128)S(1)}) fusion(s32[2048]{0:T(1024)S(1)} %fusion.67, s32[512]{0:T(512)S(1)} %iota_add_fusion.2, bf16[512,576]{1,0:T(8,128)(2,1)S(1)} %dynamic-slice_bitcast_fusion.4, bf16[2048,576]{1,0:T(8,128)(2,1)} %get-tuple-element.370), kind=kOutput, calls=%fused_computation.3.clone.1 | convolution fusion | flops 1212151808 | bytes 7161856 | tf_op jit(solution)/shard_map/while/body/eval_jaxpr/dot_general | solution.py:102
  265.6 4.6 %multiply_add_fusion.5 = f32[2048,512]{1,0:T(8,128)} fusion(f32[2048,512]{1,0:T(8,128)} %get-tuple-element.358, f32[512,2048]{1,0:T(8,128)S(1)} %get-tuple-element.301, f32[2048]{0:T(1024)S(1)} %get-tuple-element.303, f32[2048]{0:T(1024)S(1)} %max.11, s32[2048]{0:T(1024)S(1)} %fusion.67, s32[512]{0:T(512)S(1)} %iota_add_fusion.2, ...), kind=kOutput, calls=%fused_computation.4.clone.1 | convolution fusion | flops 1081081856 | bytes 13133824 | tf_op jit(solution)/shard_map/while/body/eval_jaxpr/dot_general | solution.py:111
  271.4 1.2 dynamic-slice_bitcast_fusion.4
  272.6 3.7 %fusion.68 = (f32[2048]{0:T(1024)S(1)}, f32[512,2048]{1,0:T(8,128)S(1)}) fusion(s32[2048]{0:T(1024)S(1)} %fusion.67, s32[512]{0:T(512)S(1)} %iota_add_fusion.2, bf16[512,576]{1,0:T(8,128)(2,1)S(1)} %dynamic-slice_bitcast_fusion.4, bf16[2048,576]{1,0:T(8,128)(2,1)} %get-tuple-element.370), kind=kOutput, calls=%fused_computation.3.clone.1 | convolution fusion | flops 1212151808 | bytes 7161856 | tf_op jit(solution)/shard_map/while/body/eval_jaxpr/dot_general | solution.py:102
  277.3 4.6 %multiply_add_fusion.5 = f32[2048,512]{1,0:T(8,128)} fusion(f32[2048,512]{1,0:T(8,128)} %get-tuple-element.358, f32[512,2048]{1,0:T(8,128)S(1)} %get-tuple-element.301, f32[2048]{0:T(1024)S(1)} %get-tuple-element.303, f32[2048]{0:T(1024)S(1)} %max.11, s32[2048]{0:T(1024)S(1)} %fusion.67, s32[512]{0:T(512)S(1)} %iota_add_fusion.2, ...), kind=kOutput, calls=%fused_computation.4.clone.1 | convolution fusion | flops 1081081856 | bytes 13133824 | tf_op jit(solution)/shard_map/while/body/eval_jaxpr/dot_general | solution.py:111
  283.1 1.2 dynamic-slice_bitcast_fusion.4
  284.3 3.6 %fusion.68 = (f32[2048]{0:T(1024)S(1)}, f32[512,2048]{1,0:T(8,128)S(1)}) fusion(s32[2048]{0:T(1024)S(1)} %fusion.67, s32[512]{0:T(512)S(1)} %iota_add_fusion.2, bf16[512,576]{1,0:T(8,128)(2,1)S(1)} %dynamic-slice_bitcast_fusion.4, bf16[2048,576]{1,0:T(8,128)(2,1)} %get-tuple-element.370), kind=kOutput, calls=%fused_computation.3.clone.1 | convolution fusion | flops 1212151808 | bytes 7161856 | tf_op jit(solution)/shard_map/while/body/eval_jaxpr/dot_general | solution.py:102
  289.0 4.6 %multiply_add_fusion.5 = f32[2048,512]{1,0:T(8,128)} fusion(f32[2048,512]{1,0:T(8,128)} %get-tuple-element.358, f32[512,2048]{1,0:T(8,128)S(1)} %get-tuple-element.301, f32[2048]{0:T(1024)S(1)} %get-tuple-element.303, f32[2048]{0:T(1024)S(1)} %max.11, s32[2048]{0:T(1024)S(1)} %fusion.67, s32[512]{0:T(512)S(1)} %iota_add_fusion.2, ...), kind=kOutput, calls=%fused_computation.4.clone.1 | convolution fusion | flops 1081081856 | bytes 13133824 | tf_op jit(solution)/shard_map/while/body/eval_jaxpr/dot_general | solution.py:111
  294.8 1.2 dynamic-slice_bitcast_fusion.4
  296.0 3.6 %fusion.68 = (f32[2048]{0:T(1024)S(1)}, f32[512,2048]{1,0:T(8,128)S(1)}) fusion(s32[2048]{0:T(1024)S(1)} %fusion.67, s32[512]{0:T(512)S(1)} %iota_add_fusion.2, bf16[512,576]{1,0:T(8,128)(2,1)S(1)} %dynamic-slice_bitcast_fusion.4, bf16[2048,576]{1,0:T(8,128)(2,1)} %get-tuple-element.370), kind=kOutput, calls=%fused_computation.3.clone.1 | convolution fusion | flops 1212151808 | bytes 7161856 | tf_op jit(solution)/shard_map/while/body/eval_jaxpr/dot_general | solution.py:102
  300.7 4.6 %multiply_add_fusion.5 = f32[2048,512]{1,0:T(8,128)} fusion(f32[2048,512]{1,0:T(8,128)} %get-tuple-element.358, f32[512,2048]{1,0:T(8,128)S(1)} %get-tuple-element.301, f32[2048]{0:T(1024)S(1)} %get-tuple-element.303, f32[2048]{0:T(1024)S(1)} %max.11, s32[2048]{0:T(1024)S(1)} %fusion.67, s32[512]{0:T(512)S(1)} %iota_add_fusion.2, ...), kind=kOutput, calls=%fused_computation.4.clone.1 | convolution fusion | flops 1081081856 | bytes 13133824 | tf_op jit(solution)/shard_map/while/body/eval_jaxpr/dot_general | solution.py:111
  306.5 1.2 dynamic-slice_bitcast_fusion.4
  307.7 3.7 %fusion.68 = (f32[2048]{0:T(1024)S(1)}, f32[512,2048]{1,0:T(8,128)S(1)}) fusion(s32[2048]{0:T(1024)S(1)} %fusion.67, s32[512]{0:T(512)S(1)} %iota_add_fusion.2, bf16[512,576]{1,0:T(8,128)(2,1)S(1)} %dynamic-slice_bitcast_fusion.4, bf16[2048,576]{1,0:T(8,128)(2,1)} %get-tuple-element.370), kind=kOutput, calls=%fused_computation.3.clone.1 | convolution fusion | flops 1212151808 | bytes 7161856 | tf_op jit(solution)/shard_map/while/body/eval_jaxpr/dot_general | solution.py:102
  312.4 4.6 %multiply_add_fusion.5 = f32[2048,512]{1,0:T(8,128)} fusion(f32[2048,512]{1,0:T(8,128)} %get-tuple-element.358, f32[512,2048]{1,0:T(8,128)S(1)} %get-tuple-element.301, f32[2048]{0:T(1024)S(1)} %get-tuple-element.303, f32[2048]{0:T(1024)S(1)} %max.11, s32[2048]{0:T(1024)S(1)} %fusion.67, s32[512]{0:T(512)S(1)} %iota_add_fusion.2, ...), kind=kOutput, calls=%fused_computation.4.clone.1 | convolution fusion | flops 1081081856 | bytes 13133824 | tf_op jit(solution)/shard_map/while/body/eval_jaxpr/dot_general | solution.py:111
  318.2 1.2 dynamic-slice_bitcast_fusion.4
  319.4 3.6 %fusion.68 = (f32[2048]{0:T(1024)S(1)}, f32[512,2048]{1,0:T(8,128)S(1)}) fusion(s32[2048]{0:T(1024)S(1)} %fusion.67, s32[512]{0:T(512)S(1)} %iota_add_fusion.2, bf16[512,576]{1,0:T(8,128)(2,1)S(1)} %dynamic-slice_bitcast_fusion.4, bf16[2048,576]{1,0:T(8,128)(2,1)} %get-tuple-element.370), kind=kOutput, calls=%fused_computation.3.clone.1 | convolution fusion | flops 1212151808 | bytes 7161856 | tf_op jit(solution)/shard_map/while/body/eval_jaxpr/dot_general | solution.py:102
  324.1 4.6 %multiply_add_fusion.5 = f32[2048,512]{1,0:T(8,128)} fusion(f32[2048,512]{1,0:T(8,128)} %get-tuple-element.358, f32[512,2048]{1,0:T(8,128)S(1)} %get-tuple-element.301, f32[2048]{0:T(1024)S(1)} %get-tuple-element.303, f32[2048]{0:T(1024)S(1)} %max.11, s32[2048]{0:T(1024)S(1)} %fusion.67, s32[512]{0:T(512)S(1)} %iota_add_fusion.2, ...), kind=kOutput, calls=%fused_computation.4.clone.1 | convolution fusion | flops 1081081856 | bytes 13133824 | tf_op jit(solution)/shard_map/while/body/eval_jaxpr/dot_general | solution.py:111
  328.7 2.7 divide_convert_fusion
  331.5 2.7 fusion.33
  (111 shorter events, 25.0 us)
Async XLA Ops:
  7.2 30.0 %copy-start = (bf16[16,128,512]{2,1,0:T(8,128)(2,1)S(1)}, bf16[16,128,512]{2,1,0:T(8,128)(2,1)}, u32[]{:S(2)}) copy-start(bf16[16,128,512]{2,1,0:T(8,128)(2,1)} %param.19) | copy-start | bytes 6291460
  7.2 8.6 %copy-start.2 = (bf16[128,1024]{1,0:T(8,128)(2,1)S(1)}, bf16[128,1024]{1,0:T(8,128)(2,1)}, u32[]{:S(2)}) copy-start(bf16[128,1024]{1,0:T(8,128)(2,1)} %param.18) | copy-start | bytes 786436
  7.2 8.8 %copy-start.5 = (s32[256]{0:T(256)S(1)}, s32[256]{0:T(256)}, u32[]{:S(2)}) copy-start(s32[256]{0:T(256)} %param.23) | copy-start | bytes 3076
  10.7 15.5 %all-to-all-start.1 = ((bf16[4,128,576]{1,2,0:T(8,128)(2,1)}), bf16[4,128,576]{1,2,0:T(8,128)(2,1)S(1)}, u32[]{:S(2)}, u32[]{:S(2)}) async-start(bf16[4,128,576]{1,2,0:T(8,128)(2,1)} %broadcast_in_dim.54), calls=%async_computation.1 | async-start | bytes 1179648 | tf_op jit(solution)/shard_map/all_to_all | solution.py:15
  28.9 45.7 %all-to-all-start = ((bf16[32,64,576]{2,1,0:T(8,128)(2,1)}), bf16[32,64,576]{2,1,0:T(8,128)(2,1)}, u32[]{:S(2)}, u32[]{:S(2)}) async-start(bf16[32,64,576]{2,1,0:T(8,128)(2,1)} %broadcast_in_dim.53), calls=%async_computation | async-start | bytes 5242880 | tf_op jit(solution)/shard_map/all_to_all | solution.py:15
  37.1 3.6 %copy-start.3 = (f32[512]{0:T(512)S(1)}, f32[512]{0:T(512)}, u32[]{:S(2)}) copy-start(f32[512]{0:T(512)} %param.16) | copy-start | bytes 6148
  37.1 190.4 %all-gather.2.cloned.1.call-start = ((), (), s32[]{:S(2)}) async-start(), calls=%async_computation.3 | async-start | bytes 4866048 | tf_op jit(solution)/shard_map/all_gather | solution.py:150
  74.6 80.1 %all-to-all-start.2 = ((bf16[32,8,9216]{2,1,0:T(8,128)(2,1)}), bf16[32,8,9216]{2,1,0:T(8,128)(2,1)}, u32[]{:S(2)}, u32[]{:S(2)}) async-start(bf16[32,8,9216]{2,1,0:T(8,128)(2,1)} %fusion.30), calls=%async_computation.2 | async-start | bytes 9437184 | tf_op jit(solution)/shard_map/all_to_all | solution.py:159
  90.8 3.4 %copy-start.1 = (f32[512,2048]{1,0:T(8,128)S(1)}, f32[512,2048]{1,0:T(8,128)}, u32[]{:S(2)}) copy-start(f32[512,2048]{1,0:T(8,128)} %get-tuple-element.313) | copy-start | bytes 12582916 | tf_op jit(solution)/shard_map/while
  106.0 3.5 %copy-start.1 = (f32[512,2048]{1,0:T(8,128)S(1)}, f32[512,2048]{1,0:T(8,128)}, u32[]{:S(2)}) copy-start(f32[512,2048]{1,0:T(8,128)} %get-tuple-element.313) | copy-start | bytes 12582916 | tf_op jit(solution)/shard_map/while
  122.8 3.4 %copy-start.1 = (f32[512,2048]{1,0:T(8,128)S(1)}, f32[512,2048]{1,0:T(8,128)}, u32[]{:S(2)}) copy-start(f32[512,2048]{1,0:T(8,128)} %get-tuple-element.313) | copy-start | bytes 12582916 | tf_op jit(solution)/shard_map/while
  139.6 3.5 %copy-start.1 = (f32[512,2048]{1,0:T(8,128)S(1)}, f32[512,2048]{1,0:T(8,128)}, u32[]{:S(2)}) copy-start(f32[512,2048]{1,0:T(8,128)} %get-tuple-element.313) | copy-start | bytes 12582916 | tf_op jit(solution)/shard_map/while
  328.7 2.9 copy-start.4
Sparse Core Ops, SparseCore 0:
  41.6 185.7 all-gather.1
where the time goes:
time: 344 us; the launch traced here: 342 us
  matrix products  118 us (34%)
  waiting for transfers between devices  106 us (31%)
  other arithmetic  41.8 us (12%)
  local copies, waits for them, and re-layouts  40.5 us (12%)
  starting transfers between devices  20.2 us (6%)
  between operations  14.9 us (4%)
    all_gather x1, waiting for transfers between devices, per_device(): all_keys = lax.all_gather(new_keys, 'seq', axis=0, tiled=True)  69.1 us
    dot_general x12, matrix products, attend(): lax.dot_general(weights.astype(jnp.bfloat16), key_rows[:, :LATENT], (((0,...  53.9 us
    dot_general x12, matrix products, attend(): lax.dot_general(key_rows, queries, (((1,), (1,)), ((), ())), preferred_el...  52 us
    all_to_all x2, waiting for transfers between devices, sent_to_all(): return lax.all_to_all(copies, axis, split_axis=0, concat_axis=0, tiled=True)  30.3 us
    reduce_sum x12, other arithmetic, attend(): denominator = denominator * fading + jnp.sum(weights, axis=0)  20.7 us
    squeeze x12, local copies, waits for them, and re-layouts, sweep_keys(): state, unused = lax.scan(advance, state, (blocks, starts))  13.8 us
    all_to_all x2, starting transfers between devices, sent_to_all(): return lax.all_to_all(copies, axis, split_axis=0, concat_axis=0, tiled=True)  12.7 us
    unnamed x12, local copies, waits for them, and re-layouts  8.82 us
  transfers between devices with their start and end apart: 4, of which 4 were waited for; matrix products, arithmetic and copies ran while one was open for 25% of the time, Pallas kernels for 0%

commit v1 on v0

--- a/solution.py
+++ b/solution.py
@@ -147,7 +147,9 @@
     state = sweep_keys(state, prefix_all, prefix_rule)
     pages_dev = row_count // PAGE
     page_width = PAGE * row_width
-    all_keys = lax.all_gather(new_keys, "seq", axis=0, tiled=True)
+    all_keys = jnp.concatenate(
+        lax.all_to_all(jnp.stack([new_keys] * lax.axis_size("seq")), "seq", 0, 0), axis=0
+    )
     state = sweep_keys(state, all_keys, group_rule)
     axis_size = lax.axis_size("seq")
     targets = lax.dynamic_slice_in_dim(page_table, seq_index * pages_dev, pages_dev)

time: 344 us -> 264 us (0.77)
  waiting for transfers between devices: 106 us -> 33.1 us
  local copies, waits for them, and re-layouts: 40.5 us -> 80.3 us
  matrix products: 118 us -> 84.7 us
  between operations: 14.9 us -> 1.47 us
  other arithmetic: 41.8 us -> 32 us
  starting transfers between devices: 20.2 us -> 29 us
    all_gather x1 -> x0, waiting for transfers between devices: 69.1 us -> none  [per_device(): all_keys = lax.all_gather(new_keys, 'seq', axis=0, tiled=True)]
    while x20 -> x60, local copies, waits for them, and re-layouts: 0.95 us -> 38.4 us
    dot_general x12, matrix products: 53.9 us -> 28.9 us  [attend(): lax.dot_general(weights.astype(jnp.bfloat16), key_rows[:, :LATENT], (((0,...]
    reduce_sum x12, other arithmetic: 20.7 us -> 11.3 us  [attend(): denominator = denominator * fading + jnp.sum(weights, axis=0)]
    dot_general x12, matrix products: 52 us -> 43.9 us  [attend(): lax.dot_general(key_rows, queries, (((1,), (1,)), ((), ())), preferred_el...]
    all_to_all x1, waiting for transfers between devices: 6.93 us -> 0.01 us  [per_device(): lax.all_to_all(outgoing, 'seq', split_axis=0, concat_axis=0, tiled=True)]
    all_to_all x0 -> x1, starting transfers between devices: none -> 6.71 us  [per_device(): lax.all_to_all(jnp.stack([new_keys] * lax.axis_size('seq')), 'seq', 0, 0)]
    all_to_all x0 -> x1, waiting for transfers between devices: none -> 6.24 us  [per_device(): lax.all_to_all(jnp.stack([new_keys] * lax.axis_size('seq')), 'seq', 0, 0)]
  transfers between devices with their start and end apart: 4 -> 4, of which waited for: 4 -> 3; matrix products, arithmetic and copies ran while one was open for 25% -> 56% of each run, Pallas kernels for 0% -> 0%
where the time goes in v1:
time: 264 us; the launch traced here: 262 us
  matrix products  84.7 us (32%)
  local copies, waits for them, and re-layouts  80.3 us (30%)
  waiting for transfers between devices  33.1 us (13%)
  other arithmetic  32 us (12%)
  starting transfers between devices  29 us (11%)
    dot_general x12, matrix products, attend(): lax.dot_general(key_rows, queries, (((1,), (1,)), ((), ())), preferred_el...  43.9 us
    while x60, local copies, waits for them, and re-layouts  38.4 us
    dot_general x12, matrix products, attend(): lax.dot_general(weights.astype(jnp.bfloat16), key_rows[:, :LATENT], (((0,...  28.9 us
    all_to_all x2, waiting for transfers between devices, sent_to_all(): return lax.all_to_all(copies, axis, split_axis=0, concat_axis=0, tiled=True)  26.9 us
    squeeze x12, local copies, waits for them, and re-layouts, sweep_keys(): state, unused = lax.scan(advance, state, (blocks, starts))  13.8 us
    all_to_all x2, starting transfers between devices, sent_to_all(): return lax.all_to_all(copies, axis, split_axis=0, concat_axis=0, tiled=True)  12.7 us
    reduce_sum x12, other arithmetic, attend(): denominator = denominator * fading + jnp.sum(weights, axis=0)  11.3 us
    all_to_all x1, starting transfers between devices, per_device(): lax.all_to_all(outgoing, 'seq', split_axis=0, concat_axis=0, tiled=True)  9.65 us
  transfers between devices with their start and end apart: 4, of which 3 were waited for; matrix products, arithmetic and copies ran while one was open for 56% of the time, Pallas kernels for 0%

profile of v1, /device:TPU:32, one launch (start us, length us, event | category | flops | bytes accessed | tf_op | source)
XLA Modules:
  0.0 261.5 jit_solution(4975550243524191540)
XLA Ops:
  0.7 2.6 convolution_convert_fusion.1
  4.1 4.5 %all-to-all-start.1 = ((bf16[4,128,576]{1,2,0:T(8,128)(2,1)}), bf16[4,128,576]{1,2,0:T(8,128)(2,1)S(1)}, u32[]{:S(2)}, u32[]{:S(2)}) async-start(bf16[4,128,576]{1,2,0:T(8,128)(2,1)} %broadcast_in_dim.54), calls=%async_computation.1 | async-start | bytes 1179648 | tf_op jit(solution)/shard_map/all_to_all | solution.py:15
  9.5 10.1 %all-to-all-done.1 = bf16[4,128,576]{1,2,0:T(8,128)(2,1)S(1)} async-done(((bf16[4,128,576]{1,2,0:T(8,128)(2,1)}), bf16[4,128,576]{1,2,0:T(8,128)(2,1)S(1)}, u32[]{:S(2)}, u32[]{:S(2)}) %all-to-all-start.1) | async-done | bytes 589856 | tf_op jit(solution)/shard_map/all_to_all | solution.py:15
  19.6 2.7 %broadcast_in_dim.53 = bf16[32,64,576]{2,1,0:T(8,128)(2,1)} broadcast(bf16[64,576]{1,0:T(8,128)(2,1)} %param.21), dimensions={1,2} | broadcast | bytes 2433024 | tf_op jit(solution)/shard_map/broadcast_in_dim | solution.py:14
  22.3 8.2 %all-to-all-start = ((bf16[32,64,576]{2,1,0:T(8,128)(2,1)}), bf16[32,64,576]{2,1,0:T(8,128)(2,1)}, u32[]{:S(2)}, u32[]{:S(2)}) async-start(bf16[32,64,576]{2,1,0:T(8,128)(2,1)} %broadcast_in_dim.53), calls=%async_computation | async-start | bytes 5242880 | tf_op jit(solution)/shard_map/all_to_all | solution.py:15
  30.6 3.2 %convert_bitcast_fusion = bf16[128,16,512]{0,2,1:T(8,128)(2,1)} fusion(bf16[16,128,512]{2,1,0:T(8,128)(2,1)S(1)} %copy-done, bf16[128,2048]{1,0:T(8,128)(2,1)} %param.17), kind=kOutput, calls=%fused_computation.52 | convolution fusion | flops 269484032 | bytes 4718592 | tf_op jit(solution)/shard_map/thn,hnl->thl/dot_general | solution.py:85
  34.7 3.2 %pad_maximum_fusion = bf16[128,16,576]{0,2,1:T(8,128)(2,1)} fusion(bf16[128,16,32]{0,2,1:T(8,128)(2,1)S(1)} %get-tuple-element.207, bf16[128,16,32]{0,2,1:T(8,128)(2,1)S(1)} %get-tuple-element.206, bf16[128,16,512]{0,2,1:T(8,128)(2,1)} %convert_bitcast_fusion), kind=kLoop, calls=%fused_computation.49 | loop fusion | flops 7077888 | bytes 4718592 | tf_op jit(solution)/shard_map/concatenate | solution.py:95
  37.9 4.9 %copy.55 = bf16[128,16,576]{2,1,0:T(8,128)(2,1)} copy(bf16[128,16,576]{0,2,1:T(8,128)(2,1)} %pad_maximum_fusion) | data formatting | bytes 4718592 | tf_op jit(solution)/shard_map/concatenate | solution.py:95
  42.8 3.5 %fusion.30 = bf16[32,8,9216]{2,1,0:T(8,128)(2,1)} fusion(bf16[8,9216]{1,0:T(8,128)(2,1)S(1)} %reshape.117, s32[8]{0:T(128)S(1)} %dynamic_slice.19), kind=kOutput, calls=%fused_computation.47 | convolution fusion | flops 40110080 | bytes 4866080 | tf_op jit(solution)/shard_map/dot_general | solution.py:158
  46.3 16.8 %all-to-all-done = bf16[32,64,576]{2,1,0:T(8,128)(2,1)} async-done(((bf16[32,64,576]{2,1,0:T(8,128)(2,1)}), bf16[32,64,576]{2,1,0:T(8,128)(2,1)}, u32[]{:S(2)}, u32[]{:S(2)}) %all-to-all-start) | async-done | bytes 2359328 | tf_op jit(solution)/shard_map/all_to_all | solution.py:15
  63.1 3.2 %stack.2 = bf16[32,128,576]{1,2,0:T(8,128)(2,1)} broadcast(bf16[128,576]{0,1:T(8,128)(2,1)S(1)} %pad_maximum_fusion.1), dimensions={1,2} | broadcast | bytes 4866048 | tf_op jit(solution)/shard_map/stack | solution.py:151
  66.3 6.7 %all-to-all-start.2 = ((bf16[32,128,576]{1,2,0:T(8,128)(2,1)}), bf16[32,128,576]{1,2,0:T(8,128)(2,1)}, u32[]{:S(2)}, u32[]{:S(2)}) async-start(bf16[32,128,576]{1,2,0:T(8,128)(2,1)} %stack.2), calls=%async_computation.2 | async-start | bytes 9437184 | tf_op jit(solution)/shard_map/all_to_all | solution.py:151
  73.0 52.7 %while.31 = (s32[]{:T(128)}, f32[2048]{0:T(1024)S(1)}, f32[2048]{0:T(1024)S(1)}, f32[2048,512]{1,0:T(8,128)}, s32[4]{0:T(128)S(1)}, /*index=5*/s32[]{:T(128)}, b...) while((s32[]{:T(128)}, f32[2048]{0:T(1024)S(1)}, ...), condition=%wide.region_3.4_spmd.clone, body=%wide.region_0.3_spmd.clone.sunk | while | flops 2296392704 | bytes 59312328 | solution.py:132
  73.6 1.3 add_compare_fusion.2
  76.0 3.7 %select_reduce_fusion.2 = (f32[2048]{0:T(1024)S(1)}, f32[512,2048]{1,0:T(8,128)S(1)}) fusion(pred[512]{0:T(512)(128)(4,1)S(1)} %add_compare_fusion.2, bf16[512,576]{1,0:T(8,128)(2,1)S(1)} %dynamic-slice_bitcast_fusion.5, bf16[2048,576]{1,0:T(8,128)(2,1)} %get-tuple-element.353), kind=kOutput, calls=%fused_computation.30.clone.1 | convolution fusion | flops 1211103232 | bytes 7152128 | tf_op jit(solution)/shard_map/while/body/eval_jaxpr/dot_general | solution.py:102
  80.6 1.3 copy-done.1
  81.9 2.3 fusion.76
  84.2 2.0 copy-done.2
  86.8 1.3 add_compare_fusion.2
  89.2 3.7 %select_reduce_fusion.2 = (f32[2048]{0:T(1024)S(1)}, f32[512,2048]{1,0:T(8,128)S(1)}) fusion(pred[512]{0:T(512)(128)(4,1)S(1)} %add_compare_fusion.2, bf16[512,576]{1,0:T(8,128)(2,1)S(1)} %dynamic-slice_bitcast_fusion.5, bf16[2048,576]{1,0:T(8,128)(2,1)} %get-tuple-element.353), kind=kOutput, calls=%fused_computation.30.clone.1 | convolution fusion | flops 1211103232 | bytes 7152128 | tf_op jit(solution)/shard_map/while/body/eval_jaxpr/dot_general | solution.py:102
  93.8 1.3 copy-done.1
  95.1 2.3 fusion.76
  97.4 2.0 copy-done.2
  100.0 1.3 add_compare_fusion.2
  102.4 3.7 %select_reduce_fusion.2 = (f32[2048]{0:T(1024)S(1)}, f32[512,2048]{1,0:T(8,128)S(1)}) fusion(pred[512]{0:T(512)(128)(4,1)S(1)} %add_compare_fusion.2, bf16[512,576]{1,0:T(8,128)(2,1)S(1)} %dynamic-slice_bitcast_fusion.5, bf16[2048,576]{1,0:T(8,128)(2,1)} %get-tuple-element.353), kind=kOutput, calls=%fused_computation.30.clone.1 | convolution fusion | flops 1211103232 | bytes 7152128 | tf_op jit(solution)/shard_map/while/body/eval_jaxpr/dot_general | solution.py:102
  107.0 1.3 copy-done.1
  108.3 2.3 fusion.76
  110.6 2.0 copy-done.2
  113.1 1.3 add_compare_fusion.2
  115.6 3.7 %select_reduce_fusion.2 = (f32[2048]{0:T(1024)S(1)}, f32[512,2048]{1,0:T(8,128)S(1)}) fusion(pred[512]{0:T(512)(128)(4,1)S(1)} %add_compare_fusion.2, bf16[512,576]{1,0:T(8,128)(2,1)S(1)} %dynamic-slice_bitcast_fusion.5, bf16[2048,576]{1,0:T(8,128)(2,1)} %get-tuple-element.353), kind=kOutput, calls=%fused_computation.30.clone.1 | convolution fusion | flops 1211103232 | bytes 7152128 | tf_op jit(solution)/shard_map/while/body/eval_jaxpr/dot_general | solution.py:102
  120.1 1.3 copy-done.1
  121.4 2.3 fusion.76
  123.7 2.0 copy-done.2
  125.7 6.2 %all-to-all-done.2 = bf16[32,128,576]{1,2,0:T(8,128)(2,1)} async-done(((bf16[32,128,576]{1,2,0:T(8,128)(2,1)}), bf16[32,128,576]{1,2,0:T(8,128)(2,1)}, u32[]{:S(2)}, u32[]{:S(2)}) %all-to-all-start.2) | async-done | bytes 4718624 | tf_op jit(solution)/shard_map/all_to_all | solution.py:151
  132.0 9.6 %all-to-all-start.3 = ((bf16[32,8,9216]{2,1,0:T(8,128)(2,1)}), bf16[32,8,9216]{2,1,0:T(8,128)(2,1)}, u32[]{:S(2)}, u32[]{:S(2)}) async-start(bf16[32,8,9216]{2,1,0:T(8,128)(2,1)} %fusion.30), calls=%async_computation.3 | async-start | bytes 9437184 | tf_op jit(solution)/shard_map/all_to_all | solution.py:161
  141.6 7.7 %copy.64 = bf16[32,128,576]{2,1,0:T(8,128)(2,1)} copy(bf16[32,128,576]{1,2,0:T(8,128)(2,1)} %all-to-all-done.2) | data formatting | bytes 9437184
  149.3 102.0 %while.30 = (s32[]{:T(128)}, f32[2048]{0:T(1024)S(1)}, f32[2048]{0:T(1024)S(1)}, f32[2048,512]{1,0:T(8,128)}, s32[8]{0:T(128)S(1)}, /*index=5*/bf16[8,512,576]{2...) while((s32[]{:T(128)}, f32[2048]{0:T(1024)S(1)}, f32[2048]{0:T(1024)S(1)}, ...), condition=%wide.region_9.10_spmd.clone, body=%wide.region_6.9_spmd.clone.sunk | while | flops 2298501632 | bytes 59351220 | solution.py:132
  151.7 3.7 %fusion.68 = (f32[2048]{0:T(1024)S(1)}, f32[512,2048]{1,0:T(8,128)S(1)}) fusion(s32[2048]{0:T(1024)S(1)} %fusion.67, s32[512]{0:T(512)S(1)} %iota_add_fusion.2, bf16[512,576]{1,0:T(8,128)(2,1)S(1)} %dynamic-slice_bitcast_fusion.4, bf16[2048,576]{1,0:T(8,128)(2,1)} %get-tuple-element.380), kind=kOutput, calls=%fused_computation.3.clone.1 | convolution fusion | flops 1212151808 | bytes 7161856 | tf_op jit(solution)/shard_map/while/body/eval_jaxpr/dot_general | solution.py:102
  157.5 2.5 multiply_add_fusion.5
  160.0 2.0 copy-done.4
  164.4 3.7 %fusion.68 = (f32[2048]{0:T(1024)S(1)}, f32[512,2048]{1,0:T(8,128)S(1)}) fusion(s32[2048]{0:T(1024)S(1)} %fusion.67, s32[512]{0:T(512)S(1)} %iota_add_fusion.2, bf16[512,576]{1,0:T(8,128)(2,1)S(1)} %dynamic-slice_bitcast_fusion.4, bf16[2048,576]{1,0:T(8,128)(2,1)} %get-tuple-element.380), kind=kOutput, calls=%fused_computation.3.clone.1 | convolution fusion | flops 1212151808 | bytes 7161856 | tf_op jit(solution)/shard_map/while/body/eval_jaxpr/dot_general | solution.py:102
  170.3 2.5 multiply_add_fusion.5
  172.8 2.0 copy-done.4
  177.2 3.6 %fusion.68 = (f32[2048]{0:T(1024)S(1)}, f32[512,2048]{1,0:T(8,128)S(1)}) fusion(s32[2048]{0:T(1024)S(1)} %fusion.67, s32[512]{0:T(512)S(1)} %iota_add_fusion.2, bf16[512,576]{1,0:T(8,128)(2,1)S(1)} %dynamic-slice_bitcast_fusion.4, bf16[2048,576]{1,0:T(8,128)(2,1)} %get-tuple-element.380), kind=kOutput, calls=%fused_computation.3.clone.1 | convolution fusion | flops 1212151808 | bytes 7161856 | tf_op jit(solution)/shard_map/while/body/eval_jaxpr/dot_general | solution.py:102
  183.0 2.5 multiply_add_fusion.5
  185.5 2.0 copy-done.4
  189.9 3.7 %fusion.68 = (f32[2048]{0:T(1024)S(1)}, f32[512,2048]{1,0:T(8,128)S(1)}) fusion(s32[2048]{0:T(1024)S(1)} %fusion.67, s32[512]{0:T(512)S(1)} %iota_add_fusion.2, bf16[512,576]{1,0:T(8,128)(2,1)S(1)} %dynamic-slice_bitcast_fusion.4, bf16[2048,576]{1,0:T(8,128)(2,1)} %get-tuple-element.380), kind=kOutput, calls=%fused_computation.3.clone.1 | convolution fusion | flops 1212151808 | bytes 7161856 | tf_op jit(solution)/shard_map/while/body/eval_jaxpr/dot_general | solution.py:102
  195.8 2.5 multiply_add_fusion.5
  198.3 2.0 copy-done.4
  202.7 3.6 %fusion.68 = (f32[2048]{0:T(1024)S(1)}, f32[512,2048]{1,0:T(8,128)S(1)}) fusion(s32[2048]{0:T(1024)S(1)} %fusion.67, s32[512]{0:T(512)S(1)} %iota_add_fusion.2, bf16[512,576]{1,0:T(8,128)(2,1)S(1)} %dynamic-slice_bitcast_fusion.4, bf16[2048,576]{1,0:T(8,128)(2,1)} %get-tuple-element.380), kind=kOutput, calls=%fused_computation.3.clone.1 | convolution fusion | flops 1212151808 | bytes 7161856 | tf_op jit(solution)/shard_map/while/body/eval_jaxpr/dot_general | solution.py:102
  208.5 2.5 multiply_add_fusion.5
  211.0 2.0 copy-done.4
  215.4 3.7 %fusion.68 = (f32[2048]{0:T(1024)S(1)}, f32[512,2048]{1,0:T(8,128)S(1)}) fusion(s32[2048]{0:T(1024)S(1)} %fusion.67, s32[512]{0:T(512)S(1)} %iota_add_fusion.2, bf16[512,576]{1,0:T(8,128)(2,1)S(1)} %dynamic-slice_bitcast_fusion.4, bf16[2048,576]{1,0:T(8,128)(2,1)} %get-tuple-element.380), kind=kOutput, calls=%fused_computation.3.clone.1 | convolution fusion | flops 1212151808 | bytes 7161856 | tf_op jit(solution)/shard_map/while/body/eval_jaxpr/dot_general | solution.py:102
  221.3 2.5 multiply_add_fusion.5
  223.8 2.0 copy-done.4
  228.2 3.6 %fusion.68 = (f32[2048]{0:T(1024)S(1)}, f32[512,2048]{1,0:T(8,128)S(1)}) fusion(s32[2048]{0:T(1024)S(1)} %fusion.67, s32[512]{0:T(512)S(1)} %iota_add_fusion.2, bf16[512,576]{1,0:T(8,128)(2,1)S(1)} %dynamic-slice_bitcast_fusion.4, bf16[2048,576]{1,0:T(8,128)(2,1)} %get-tuple-element.380), kind=kOutput, calls=%fused_computation.3.clone.1 | convolution fusion | flops 1212151808 | bytes 7161856 | tf_op jit(solution)/shard_map/while/body/eval_jaxpr/dot_general | solution.py:102
  234.0 2.5 multiply_add_fusion.5
  236.5 2.0 copy-done.4
  240.9 3.7 %fusion.68 = (f32[2048]{0:T(1024)S(1)}, f32[512,2048]{1,0:T(8,128)S(1)}) fusion(s32[2048]{0:T(1024)S(1)} %fusion.67, s32[512]{0:T(512)S(1)} %iota_add_fusion.2, bf16[512,576]{1,0:T(8,128)(2,1)S(1)} %dynamic-slice_bitcast_fusion.4, bf16[2048,576]{1,0:T(8,128)(2,1)} %get-tuple-element.380), kind=kOutput, calls=%fused_computation.3.clone.1 | convolution fusion | flops 1212151808 | bytes 7161856 | tf_op jit(solution)/shard_map/while/body/eval_jaxpr/dot_general | solution.py:102
  246.8 2.5 multiply_add_fusion.5
  249.3 2.0 copy-done.4
  251.3 2.7 %divide_convert_fusion = bf16[2048,512]{1,0:T(8,128)(2,1)S(1)} fusion(f32[2048,512]{1,0:T(8,128)} %get-tuple-element.92, f32[2048]{0:T(1024)S(1)} %get-tuple-element.93), kind=kLoop, calls=%fused_computation.48 | loop fusion | flops 2097152 | bytes 6299648 | tf_op jit(solution)/shard_map/convert_element_type | solution.py:167
  254.1 2.7 %fusion.33 = bf16[16,128,128]{1,2,0:T(8,128)(2,1)S(1)} fusion(bf16[16,512,128]{2,1,0:T(8,128)(2,1)S(1)} %copy-done.7, bf16[128,16,512]{2,1,0:T(8,128)(2,1)S(1)} %bitcast.54), kind=kOutput, calls=%fused_computation.53 | convolution fusion | flops 268697600 | bytes 4718592 | tf_op jit(solution)/shard_map/thl,hlv->thv/dot_general | solution.py:169
  257.8 3.7 %reduce_sum.50 = bf16[8,9216]{1,0:T(8,128)(2,1)} reduce(bf16[32,8,9216]{2,1,0:T(8,128)(2,1)} %all-to-all-done.3, bf16[]{:T(256)} %constant.81.clone.1), dimensions={0}, to_apply=%region_10.11 | reduce | flops 2285568 | bytes 4866050 | tf_op jit(solution)/shard_map/reduce_sum | solution.py:162
  (151 shorter events, 50.1 us)
Async XLA Ops:
  0.6 30.0 %copy-start = (bf16[16,128,512]{2,1,0:T(8,128)(2,1)S(1)}, bf16[16,128,512]{2,1,0:T(8,128)(2,1)}, u32[]{:S(2)}) copy-start(bf16[16,128,512]{2,1,0:T(8,128)(2,1)} %param.19) | copy-start | bytes 6291460
  0.6 8.6 %copy-start.5 = (bf16[128,1024]{1,0:T(8,128)(2,1)S(1)}, bf16[128,1024]{1,0:T(8,128)(2,1)}, u32[]{:S(2)}) copy-start(bf16[128,1024]{1,0:T(8,128)(2,1)} %param.18) | copy-start | bytes 786436
  0.7 8.8 %copy-start.8 = (s32[256]{0:T(256)S(1)}, s32[256]{0:T(256)}, u32[]{:S(2)}) copy-start(s32[256]{0:T(256)} %param.23) | copy-start | bytes 3076
  4.1 15.5 %all-to-all-start.1 = ((bf16[4,128,576]{1,2,0:T(8,128)(2,1)}), bf16[4,128,576]{1,2,0:T(8,128)(2,1)S(1)}, u32[]{:S(2)}, u32[]{:S(2)}) async-start(bf16[4,128,576]{1,2,0:T(8,128)(2,1)} %broadcast_in_dim.54), calls=%async_computation.1 | async-start | bytes 1179648 | tf_op jit(solution)/shard_map/all_to_all | solution.py:15
  22.3 40.8 %all-to-all-start = ((bf16[32,64,576]{2,1,0:T(8,128)(2,1)}), bf16[32,64,576]{2,1,0:T(8,128)(2,1)}, u32[]{:S(2)}, u32[]{:S(2)}) async-start(bf16[32,64,576]{2,1,0:T(8,128)(2,1)} %broadcast_in_dim.53), calls=%async_computation | async-start | bytes 5242880 | tf_op jit(solution)/shard_map/all_to_all | solution.py:15
  30.5 3.5 %copy-start.6 = (f32[512]{0:T(512)S(1)}, f32[512]{0:T(512)}, u32[]{:S(2)}) copy-start(f32[512]{0:T(512)} %param.16) | copy-start | bytes 6148
  66.3 65.7 %all-to-all-start.2 = ((bf16[32,128,576]{1,2,0:T(8,128)(2,1)}), bf16[32,128,576]{1,2,0:T(8,128)(2,1)}, u32[]{:S(2)}, u32[]{:S(2)}) async-start(bf16[32,128,576]{1,2,0:T(8,128)(2,1)} %stack.2), calls=%async_computation.2 | async-start | bytes 9437184 | tf_op jit(solution)/shard_map/all_to_all | solution.py:151
  79.7 2.2 copy-start.1
  84.2 2.0 copy-start.2
  92.9 2.2 copy-start.1
  97.4 2.0 copy-start.2
  106.1 2.2 copy-start.1
  110.5 2.0 copy-start.2
  119.2 2.2 copy-start.1
  123.7 2.0 copy-start.2
  132.0 125.9 %all-to-all-start.3 = ((bf16[32,8,9216]{2,1,0:T(8,128)(2,1)}), bf16[32,8,9216]{2,1,0:T(8,128)(2,1)}, u32[]{:S(2)}, u32[]{:S(2)}) async-start(bf16[32,8,9216]{2,1,0:T(8,128)(2,1)} %fusion.30), calls=%async_computation.3 | async-start | bytes 9437184 | tf_op jit(solution)/shard_map/all_to_all | solution.py:161
  155.3 2.2 copy-start.3
  160.0 2.0 copy-start.4
  168.1 2.2 copy-start.3
  172.8 2.0 copy-start.4
  180.8 2.2 copy-start.3
  185.5 2.0 copy-start.4
  193.6 2.2 copy-start.3
  198.3 2.0 copy-start.4
  206.3 2.2 copy-start.3
  211.0 2.0 copy-start.4
  219.1 2.2 copy-start.3
  223.8 2.0 copy-start.4
  231.8 2.2 copy-start.3
  236.5 2.0 copy-start.4
  244.6 2.2 copy-start.3
  249.3 2.0 copy-start.4
  251.3 2.9 %copy-start.7 = (bf16[16,512,128]{2,1,0:T(8,128)(2,1)S(1)}, bf16[16,512,128]{2,1,0:T(8,128)(2,1)}, u32[]{:S(2)}) copy-start(bf16[16,512,128]{2,1,0:T(8,128)(2,1)} %param.20) | copy-start | bytes 6291460
